TPU v7x, 32 devices: a whole 2x2x4 slice. The times are simulated.
32 devices in a mesh: blk: 4 (over y, x), rep: 8 (over z, core).
Axes of the slice: x: 2, y: 2, z: 4, core: 2. Of those that a mesh axis runs over, the one named last changes fastest.
Arguments:
- query_hidden: bfloat16 [8, 16, 32, 768], P('rep', 'blk'), may hold values from -18 to 18
- passage_hidden: bfloat16 [8, 16, 512, 768], P('rep', 'blk'), may hold values from -6 to 6
- lengths: int32 [8, 16], P('rep', 'blk'), may hold values from 64 to 512
- projection: bfloat16 [768, 128], replicated, may hold values from -0.21875 to 0.21875
Outputs:
- query_grad: float32 [8, 16, 32, 128], P('rep', 'blk')
- passage_grad: float32 [8, 16, 512, 128], P('rep', 'blk')
- grad_weight: float32 [768, 128], replicated
- loss: float32 [], replicated
All inputs are finite; a program needn't handle non-finite values.
Results may differ from a plain program's by a relative error of at most 0.0097.
Values may be sent and summed in bfloat16 or wider, within the bound.
A program may use at most 128 MiB of HBM per device.

v0:
```python
import jax
import jax.numpy as jnp
from jax import lax
from jax.sharding import PartitionSpec as P

temper = 0.5


def soft_scores(scores, lens):
    slots = scores.shape[-1]
    valid = lax.broadcasted_iota(jnp.int32, (lens.shape[0], slots), 1) < lens[:, None]
    scaled = jnp.where(valid[None], scores / temper, -jnp.inf)
    top = jnp.max(scaled, -1, keepdims=True)
    logz = top + jnp.log(jnp.sum(jnp.exp(scaled - top), -1, keepdims=True))
    pooled = temper * (logz[..., 0] - jnp.log(lens.astype(jnp.float32))[None])
    return (pooled, scaled, logz)


def cross_entropy(score, first, total):
    top = jnp.max(score, 1, keepdims=True)
    lse = top + jnp.log(jnp.sum(jnp.exp(score - top), 1, keepdims=True))
    target = lax.broadcasted_iota(jnp.int32, score.shape, 1) == first + lax.broadcasted_iota(
        jnp.int32, score.shape, 0
    )
    loss_part = jnp.sum(lse[:, 0] - jnp.sum(jnp.where(target, score, 0.0), 1))
    dscore = (jnp.exp(score - lse) - target.astype(jnp.float32)) / total
    return (loss_part, dscore)


def weighted(dscore, scaled, logz, qlen):
    spread = jnp.repeat(dscore, qlen, axis=0)
    grad_a = (spread[:, :, None] * jnp.exp(scaled - logz)).astype(jnp.bfloat16)
    return grad_a.reshape(grad_a.shape[0], -1)


def shards(query_hidden, passage_hidden, lengths, projection):
    hidden = projection.shape[0]
    nquery = query_hidden.shape[1]
    qlen = query_hidden.shape[2]
    npass = passage_hidden.shape[1]
    plen = passage_hidden.shape[2]
    groups = lax.axis_size("blk")
    total = groups * lax.axis_size("rep") * nquery
    first = lax.axis_index("blk") * nquery
    qflat = query_hidden[0].reshape(-1, hidden)
    pflat = passage_hidden[0].reshape(-1, hidden)
    qtok = jnp.dot(qflat, projection, preferred_element_type=jnp.float32).astype(jnp.bfloat16)
    ptok = jnp.dot(pflat, projection, preferred_element_type=jnp.float32).astype(jnp.bfloat16)
    every_tok = lax.all_gather(qtok, "blk", axis=0, tiled=True)
    scores = jnp.dot(every_tok, ptok.T, preferred_element_type=jnp.float32).reshape(
        groups * nquery * qlen, npass, plen
    )
    pooled, scaled, logz = soft_scores(scores, lengths[0])
    block_score = jnp.sum(pooled.reshape(groups * nquery, qlen, npass), 1)
    score = lax.all_to_all(block_score, "blk", split_axis=0, concat_axis=1, tiled=True)
    loss_part, dscore = cross_entropy(score, first, total)
    block_grad = lax.all_to_all(dscore, "blk", split_axis=1, concat_axis=0, tiled=True)
    grad_a = weighted(block_grad, scaled, logz, qlen)
    pgrad = jnp.dot(grad_a.T, every_tok, preferred_element_type=jnp.float32)
    qgrad = lax.psum_scatter(
        jnp.dot(grad_a, ptok, preferred_element_type=jnp.float32),
        "blk",
        scatter_dimension=0,
        tiled=True,
    )
    wgrad = jnp.dot(qflat.T, qgrad.astype(jnp.bfloat16), preferred_element_type=jnp.float32)
    wgrad = wgrad + jnp.dot(pflat.T, pgrad.astype(jnp.bfloat16), preferred_element_type=jnp.float32)
    wgrad, loss_sum = lax.psum((wgrad, loss_part), ("blk", "rep"))
    query_grad = qgrad.reshape(1, nquery, qlen, -1)
    passage_grad = pgrad.reshape(1, npass, plen, -1)
    return (query_grad, passage_grad, wgrad, loss_sum / total)


def solution(mesh):
    return jax.shard_map(
        shards,
        mesh=mesh,
        in_specs=(P("rep", "blk", None, None), P("rep", "blk", None, None), P("rep", "blk"), P()),
        out_specs=(P("rep", "blk", None, None), P("rep", "blk", None, None), P(), P()),
        check_vma=False,
    )
```

profile of v0, /device:TPU:0, one launch (start us, length us, event | category | flops | bytes accessed | tf_op | source)
XLA Modules:
  0.0 233.2 jit_solution(2799079594073589666)
XLA Ops:
  7.2 0.0 copy-start
  7.2 0.0 copy-start.8
  7.2 0.0 copy-start.9
  7.2 1.9 copy-done
  9.1 1.9 convolution_convert_fusion
  11.0 0.0 copy-start.6
  11.0 0.0 copy-done.8
  11.0 0.0 copy-done.9
  11.0 0.2 convolution_convert_fusion.1
  11.2 9.9 %all_gather.3 = bf16[512,128]{1,0:T(8,128)(2,1)S(1)} all-gather(bf16[128,128]{1,0:T(8,128)(2,1)S(1)} %convolution_convert_fusion.1), channel_id=1, replica_groups=mesh['blk'=4,'rep'=8] {'blk'}, dimensions={0}, use_global_device_ids=true | all-gather | bytes 163840 | tf_op jit(solution)/shard_map/all_gather | solution.py:49
  21.1 0.0 copy-done.6
  21.2 2.6 %convolution_multiply_fusion = f32[512,2048]{1,0:T(8,128)} fusion(bf16[512,128]{1,0:T(8,128)(2,1)S(1)} %all_gather.3, bf16[2048,128]{1,0:T(8,128)(2,1)S(1)} %convolution_convert_fusion), kind=kOutput, calls=%fused_computation.3 | convolution fusion | flops 269484032 | bytes 4849664 | tf_op jit(solution)/shard_map/dot_general | solution.py:50
  23.8 0.0 copy-start.11
  23.8 6.0 %div.19 = f32[512,4,512]{2,1,0:T(4,128)} reshape(f32[512,2048]{1,0:T(8,128)} %convolution_multiply_fusion) | data formatting | bytes 8388608 | tf_op jit(solution)/shard_map/div | solution.py:12
  29.8 0.0 copy-done.11
  29.8 0.1 iota_compare_fusion
  29.9 3.3 %select_reduce_fusion = f32[512,4]{1,0:T(8,128)S(1)} fusion(f32[512,4,512]{2,1,0:T(4,128)} %div.19, pred[4,512]{1,0:T(4,128)(4,1)S(1)} %iota_compare_fusion), kind=kLoop, calls=%fused_computation.2 | loop fusion | flops 2095104 | bytes 4204544 | tf_op jit(solution)/shard_map/reduce_max | solution.py:13
  33.2 0.1 copy-done.1
  33.3 2.6 %exponential_reduce_fusion = f32[512,4]{1,0:T(8,128)S(1)} fusion(f32[512,4,512]{2,1,0:T(4,128)S(1)} %copy-done.1, f32[512,4]{1,0:T(8,128)S(1)} %select_reduce_fusion, pred[4,512]{1,0:T(4,128)(4,1)S(1)} %iota_compare_fusion), kind=kLoop, calls=%fused_computation.1 | loop fusion | flops 3143680 | bytes 4212736 | tf_op jit(solution)/shard_map/reduce_sum | solution.py:14
  35.9 0.1 multiply_reduce_fusion
  36.0 0.7 copy.11
  36.7 3.2 %all-to-all-start = ((f32[4,4,4]{1,2,0:T(4,128)}), f32[4,4,4]{1,2,0:T(4,128)S(1)}, u32[]{:S(2)}, u32[]{:S(2)}) async-start(f32[4,4,4]{1,2,0:T(4,128)} %copy.11), calls=%async_computation | async-start | bytes 16384 | tf_op jit(solution)/shard_map/all_to_all | solution.py:55
  40.0 0.6 multiply_add_fusion
  40.5 0.5 iota_add_fusion
  41.1 0.7 sub.65
  41.8 0.0 copy-start.10
  41.8 0.0 copy-start.13
  41.8 0.0 copy-start.12
  41.8 3.9 %copy.21 = f32[64,8,4,512]{3,1,2,0:T(8,128)} copy(f32[64,8,4,512]{3,2,1,0:T(4,128)S(1)} %bitcast.49) | data formatting | bytes 8388608
  45.7 0.0 all-to-all-done
  45.7 0.0 copy-done.10
  45.8 0.0 copy-done.13
  45.8 0.1 fusion.6
  45.8 0.6 subtract_reduce_fusion
  46.5 0.7 fusion.5
  47.1 4.2 %all-to-all-start.1 = ((f32[4,4,4]{0,2,1:T(4,128)}), f32[4,4,4]{0,2,1:T(4,128)S(1)}, u32[]{:S(2)}, u32[]{:S(2)}) async-start(f32[4,4,4]{0,2,1:T(4,128)} %fusion.5), calls=%async_computation.1 | async-start | bytes 16384 | tf_op jit(solution)/shard_map/all_to_all | solution.py:57
  51.3 0.0 reduce-scatter.2.cloned.1.call-start
  51.3 0.0 copy-done.12
  51.3 0.1 lt.24
  51.4 4.6 %all-to-all-done.1 = f32[4,4,4]{0,2,1:T(4,128)S(1)} async-done(((f32[4,4,4]{0,2,1:T(4,128)}), f32[4,4,4]{0,2,1:T(4,128)S(1)}, u32[]{:S(2)}, u32[]{:S(2)}) %all-to-all-start.1) | async-done | bytes 288 | tf_op jit(solution)/shard_map/all_to_all | solution.py:57
  56.0 0.1 copy.17
  56.1 0.7 mul.27
  56.8 0.0 copy-start.2
  56.8 0.0 copy-start.4
  56.9 2.0 copy.19
  58.9 0.1 copy-done.2
  59.0 1.3 copy-done.4
  60.3 1.6 multiply_convert_fusion
  61.9 0.0 copy-start.3
  61.9 1.3 copy-done.3
  63.2 0.0 copy-done.7
  63.2 1.4 fusion.10
  64.6 0.0 reduce-scatter.2.cloned.1.call-update
  64.7 0.0 all-reduce.2.cloned.1.call-start
  64.7 2.3 fusion.11
  67.0 0.0 copy-start.5
  67.0 1.0 copy-done.5
  68.0 0.6 fusion.1
  68.6 19.9 %reduce-scatter.2.cloned.1.call-done = f32[128,128]{1,0:T(8,128)} async-done(((f32[512,128]{1,0:T(8,128)}), f32[128,128]{1,0:T(8,128)}) %reduce-scatter.2.cloned.1.call-update) | async-done | bytes 65552 | tf_op jit(solution)/shard_map/reduce_scatter | solution.py:60
  88.5 1.9 fusion
  90.5 0.0 all-reduce.2.cloned.1.call-update
  90.5 39.6 %psum.15 = f32[]{:T(128)} all-reduce(f32[]{:T(128)} %get-tuple-element.14), channel_id=1, replica_groups=mesh['blk'=4,'rep'=8] {'blk','rep'}, use_global_device_ids=true, to_apply=%region_9.10 | all-reduce | flops 1 | bytes 8 | tf_op jit(solution)/shard_map/psum | solution.py:68
  130.7 92.6 %all-reduce.2.cloned.1.call-done = f32[768,128]{0,1:T(8,128)} async-done(((f32[768,128]{0,1:T(8,128)}), f32[768,128]{0,1:T(8,128)}) %all-reduce.2.cloned.1.call-update) | async-done | bytes 393232 | tf_op jit(solution)/shard_map/psum | solution.py:68
  223.3 1.9 copy.14
  (8 shorter events, 0.1 us)
Async XLA Ops:
  7.2 1.9 copy-start
  7.2 3.8 %copy-start.8 = (bf16[768,128]{1,0:T(8,128)(2,1)S(1)}, bf16[768,128]{1,0:T(8,128)(2,1)}, u32[]{:S(2)}) copy-start(bf16[768,128]{1,0:T(8,128)(2,1)} %param.7) | copy-start | bytes 589828
  7.2 3.8 %copy-start.9 = (bf16[1,4,32,768]{3,2,1,0:T(8,128)(2,1)S(1)}, bf16[1,4,32,768]{3,2,1,0:T(8,128)(2,1)}, u32[]{:S(2)}) copy-start(bf16[1,4,32,768]{3,2,1,0:T(8,128)(2,1)} %param.4) | copy-start | bytes 589828
  11.0 10.2 %copy-start.6 = (bf16[2048,128]{1,0:T(8,128)(2,1)}, bf16[2048,128]{1,0:T(8,128)(2,1)S(1)}, u32[]{:S(2)}) copy-start(bf16[2048,128]{1,0:T(8,128)(2,1)S(1)} %convolution_convert_fusion) | copy-start | bytes 1572868
  23.8 6.0 %copy-start.11 = (s32[1,4]{1,0:T(1,128)S(1)}, s32[1,4]{1,0:T(1,128)}, u32[]{:S(2)}) copy-start(s32[1,4]{1,0:T(1,128)} %param.6) | copy-start | bytes 52
  29.8 3.4 %copy-start.1 = (f32[512,4,512]{2,1,0:T(4,128)S(1)}, f32[512,4,512]{2,1,0:T(4,128)}, u32[]{:S(2)}) copy-start(f32[512,4,512]{2,1,0:T(4,128)} %div.19) | copy-start | bytes 12582916
  36.7 9.0 %all-to-all-start = ((f32[4,4,4]{1,2,0:T(4,128)}), f32[4,4,4]{1,2,0:T(4,128)S(1)}, u32[]{:S(2)}, u32[]{:S(2)}) async-start(f32[4,4,4]{1,2,0:T(4,128)} %copy.11), calls=%async_computation | async-start | bytes 16384 | tf_op jit(solution)/shard_map/all_to_all | solution.py:55
  41.8 4.0 %copy-start.10 = (s32[4,4]{1,0:T(4,128)S(1)}, s32[4,4]{1,0:T(4,128)}, u32[]{:S(2)}) copy-start(s32[4,4]{1,0:T(4,128)} %multiply_add_fusion) | copy-start | bytes 196
  41.8 4.0 %copy-start.13 = (s32[4]{0:T(128)S(1)}, s32[4]{0:T(128)}, u32[]{:S(2)}) copy-start(s32[4]{0:T(128)} %iota_add_fusion) | copy-start | bytes 52
  41.8 9.5 %copy-start.12 = (s32[1,4]{1,0:T(1,128)S(1)}, s32[1,4]{1,0:T(1,128)}, u32[]{:S(2)}) copy-start(s32[1,4]{1,0:T(1,128)} %param.6) | copy-start | bytes 52
  47.1 8.8 %all-to-all-start.1 = ((f32[4,4,4]{0,2,1:T(4,128)}), f32[4,4,4]{0,2,1:T(4,128)S(1)}, u32[]{:S(2)}, u32[]{:S(2)}) async-start(f32[4,4,4]{0,2,1:T(4,128)} %fusion.5), calls=%async_computation.1 | async-start | bytes 16384 | tf_op jit(solution)/shard_map/all_to_all | solution.py:57
  51.3 37.2 %reduce-scatter.2.cloned.1.call-start = ((), (), s32[]{:S(2)}) async-start(), calls=%async_computation.3 | async-start | bytes 327680 | tf_op jit(solution)/shard_map/reduce_scatter | solution.py:60
  56.8 2.2 copy-start.2
  56.8 3.5 %copy-start.4 = (f32[64,8,4,512]{3,1,2,0:T(8,128)S(1)}, f32[64,8,4,512]{3,1,2,0:T(8,128)}, u32[]{:S(2)}) copy-start(f32[64,8,4,512]{3,1,2,0:T(8,128)} %copy.21) | copy-start | bytes 12582916
  60.3 2.9 %copy-start.7 = (bf16[2048,128]{1,0:T(8,128)(2,1)S(1)}, bf16[2048,128]{1,0:T(8,128)(2,1)}, u32[]{:S(2)}) copy-start(bf16[2048,128]{1,0:T(8,128)(2,1)} %copy-done.6) | copy-start | bytes 1572868
  61.9 1.4 copy-start.3
  64.7 158.7 %all-reduce.2.cloned.1.call-start = ((), (), s32[]{:S(2)}) async-start(), calls=%async_computation.4 | async-start | bytes 786432 | tf_op jit(solution)/shard_map/psum | solution.py:68
  67.0 1.0 copy-start.5
Sparse Core Ops, SparseCore 0:
  64.8 23.6 reduce-scatter.1
  94.4 128.9 all-reduce.1
where the time goes:
time: 234 us; the launch traced here: 233 us
  waiting for transfers between devices  117 us (50%)
  blocking collectives  49.5 us (21%)
  local copies, waits for them, and re-layouts  21.9 us (9%)
  between operations  16 us (7%)
  matrix products  11 us (5%)
  other arithmetic  10.1 us (4%)
  starting transfers between devices  7.45 us (3%)
    psum x1, waiting for transfers between devices, shards(): wgrad, loss_sum = lax.psum((wgrad, loss_part), ('blk', 'rep'))  92.6 us
    psum x1, blocking collectives, shards(): wgrad, loss_sum = lax.psum((wgrad, loss_part), ('blk', 'rep'))  39.6 us
    reduce_scatter x1, waiting for transfers between devices, shards(): lax.psum_scatter(jnp.dot(grad_a, ptok, preferred_element_type=jnp.float32...  19.9 us
    unnamed x33, local copies, waits for them, and re-layouts  13.6 us
    all_gather x1, blocking collectives, shards(): every_tok = lax.all_gather(qtok, 'blk', axis=0, tiled=True)  9.94 us
    div x1, local copies, waits for them, and re-layouts, soft_scores(): scaled = jnp.where(valid[None], scores / temper, -jnp.inf)  6.03 us
  transfers between devices with their start and end apart: 4, of which 3 were waited for; matrix products, arithmetic and copies ran while one was open for 4% of the time, Pallas kernels for 0%

commit v1 on v0

--- a/solution.py
+++ b/solution.py
@@ -65,7 +65,7 @@
     )
     wgrad = jnp.dot(qflat.T, qgrad.astype(jnp.bfloat16), preferred_element_type=jnp.float32)
     wgrad = wgrad + jnp.dot(pflat.T, pgrad.astype(jnp.bfloat16), preferred_element_type=jnp.float32)
-    wgrad, loss_sum = lax.psum((wgrad, loss_part), ("blk", "rep"))
+    wgrad, loss_sum = lax.psum(lax.psum((wgrad, loss_part), "rep"), "blk")
     query_grad = qgrad.reshape(1, nquery, qlen, -1)
     passage_grad = pgrad.reshape(1, npass, plen, -1)
     return (query_grad, passage_grad, wgrad, loss_sum / total)

time: 234 us -> 204 us (0.87)
  waiting for transfers between devices: 117 us -> 102 us
  blocking collectives: 49.5 us -> 34.7 us
    psum x1 -> x2, waiting for transfers between devices: 92.6 us -> 77.5 us  [shards(): wgrad, loss_sum = lax.psum(lax.psum((wgrad, loss_part), 'rep'), 'blk')]
    psum x1 -> x2, blocking collectives: 39.6 us -> 24.8 us  [shards(): wgrad, loss_sum = lax.psum(lax.psum((wgrad, loss_part), 'rep'), 'blk')]
  transfers between devices with their start and end apart: 4 -> 5, of which waited for: 3 -> 4; matrix products, arithmetic and copies ran while one was open for 4% -> 4% of each run, Pallas kernels for 0% -> 0%
where the time goes in v1:
time: 204 us; the launch traced here: 203 us
  waiting for transfers between devices  102 us (50%)
  blocking collectives  34.7 us (17%)
  local copies, waits for them, and re-layouts  21.9 us (11%)
  between operations  15.7 us (8%)
  matrix products  11 us (5%)
  other arithmetic  10.1 us (5%)
  starting transfers between devices  7.49 us (4%)
    psum x2, waiting for transfers between devices, shards(): wgrad, loss_sum = lax.psum(lax.psum((wgrad, loss_part), 'rep'), 'blk')  77.5 us
    psum x2, blocking collectives, shards(): wgrad, loss_sum = lax.psum(lax.psum((wgrad, loss_part), 'rep'), 'blk')  24.8 us
    reduce_scatter x1, waiting for transfers between devices, shards(): lax.psum_scatter(jnp.dot(grad_a, ptok, preferred_element_type=jnp.float32...  19.9 us
    unnamed x33, local copies, waits for them, and re-layouts  13.6 us
    all_gather x1, blocking collectives, shards(): every_tok = lax.all_gather(qtok, 'blk', axis=0, tiled=True)  9.94 us
    div x1, local copies, waits for them, and re-layouts, soft_scores(): scaled = jnp.where(valid[None], scores / temper, -jnp.inf)  6.03 us
    all_to_all x1, waiting for transfers between devices, shards(): lax.all_to_all(dscore, 'blk', split_axis=1, concat_axis=0, tiled=True)  4.6 us
    all_to_all x1, starting transfers between devices, shards(): lax.all_to_all(dscore, 'blk', split_axis=1, concat_axis=0, tiled=True)  4.15 us
  transfers between devices with their start and end apart: 5, of which 4 were waited for; matrix products, arithmetic and copies ran while one was open for 4% of the time, Pallas kernels for 0%

profile of v1, /device:TPU:0, one launch (start us, length us, event | category | flops | bytes accessed | tf_op | source)
XLA Modules:
  0.0 203.1 jit_solution(9297494452505017876)
XLA Ops:
  7.2 0.0 copy-start
  7.2 0.0 copy-start.8
  7.2 0.0 copy-start.9
  7.2 1.9 copy-done
  9.1 1.9 convolution_convert_fusion
  11.0 0.0 copy-start.6
  11.0 0.0 copy-done.8
  11.0 0.0 copy-done.9
  11.0 0.2 convolution_convert_fusion.1
  11.2 9.9 %all_gather.3 = bf16[512,128]{1,0:T(8,128)(2,1)S(1)} all-gather(bf16[128,128]{1,0:T(8,128)(2,1)S(1)} %convolution_convert_fusion.1), channel_id=1, replica_groups=mesh['blk'=4,'rep'=8] {'blk'}, dimensions={0}, use_global_device_ids=true | all-gather | bytes 163840 | tf_op jit(solution)/shard_map/all_gather | solution.py:49
  21.1 0.0 copy-done.6
  21.2 2.6 %convolution_multiply_fusion = f32[512,2048]{1,0:T(8,128)} fusion(bf16[512,128]{1,0:T(8,128)(2,1)S(1)} %all_gather.3, bf16[2048,128]{1,0:T(8,128)(2,1)S(1)} %convolution_convert_fusion), kind=kOutput, calls=%fused_computation.3 | convolution fusion | flops 269484032 | bytes 4849664 | tf_op jit(solution)/shard_map/dot_general | solution.py:50
  23.8 6.0 %div.19 = f32[512,4,512]{2,1,0:T(4,128)} reshape(f32[512,2048]{1,0:T(8,128)} %convolution_multiply_fusion) | data formatting | bytes 8388608 | tf_op jit(solution)/shard_map/div | solution.py:12
  29.8 0.0 copy-done.11
  29.8 0.1 iota_compare_fusion
  29.9 3.3 %select_reduce_fusion = f32[512,4]{1,0:T(8,128)S(1)} fusion(f32[512,4,512]{2,1,0:T(4,128)} %div.19, pred[4,512]{1,0:T(4,128)(4,1)S(1)} %iota_compare_fusion), kind=kLoop, calls=%fused_computation.2 | loop fusion | flops 2095104 | bytes 4204544 | tf_op jit(solution)/shard_map/reduce_max | solution.py:13
  33.2 0.1 copy-done.1
  33.3 2.6 %exponential_reduce_fusion = f32[512,4]{1,0:T(8,128)S(1)} fusion(f32[512,4,512]{2,1,0:T(4,128)S(1)} %copy-done.1, f32[512,4]{1,0:T(8,128)S(1)} %select_reduce_fusion, pred[4,512]{1,0:T(4,128)(4,1)S(1)} %iota_compare_fusion), kind=kLoop, calls=%fused_computation.1 | loop fusion | flops 3143680 | bytes 4212736 | tf_op jit(solution)/shard_map/reduce_sum | solution.py:14
  35.9 0.1 multiply_reduce_fusion
  36.0 0.7 copy.11
  36.7 3.2 %all-to-all-start = ((f32[4,4,4]{1,2,0:T(4,128)}), f32[4,4,4]{1,2,0:T(4,128)S(1)}, u32[]{:S(2)}, u32[]{:S(2)}) async-start(f32[4,4,4]{1,2,0:T(4,128)} %copy.11), calls=%async_computation | async-start | bytes 16384 | tf_op jit(solution)/shard_map/all_to_all | solution.py:55
  40.0 0.6 multiply_add_fusion
  40.5 0.5 iota_add_fusion
  41.1 0.7 sub.65
  41.8 0.0 copy-start.10
  41.8 0.0 copy-start.13
  41.8 0.0 copy-start.12
  41.8 3.9 %copy.21 = f32[64,8,4,512]{3,1,2,0:T(8,128)} copy(f32[64,8,4,512]{3,2,1,0:T(4,128)S(1)} %bitcast.49) | data formatting | bytes 8388608
  45.7 0.0 all-to-all-done
  45.7 0.0 copy-done.10
  45.8 0.0 copy-done.13
  45.8 0.1 fusion.6
  45.8 0.6 subtract_reduce_fusion
  46.5 0.7 fusion.5
  47.1 4.2 %all-to-all-start.1 = ((f32[4,4,4]{0,2,1:T(4,128)}), f32[4,4,4]{0,2,1:T(4,128)S(1)}, u32[]{:S(2)}, u32[]{:S(2)}) async-start(f32[4,4,4]{0,2,1:T(4,128)} %fusion.5), calls=%async_computation.1 | async-start | bytes 16384 | tf_op jit(solution)/shard_map/all_to_all | solution.py:57
  51.3 0.0 reduce-scatter.2.cloned.1.call-start
  51.3 0.0 copy-done.12
  51.3 0.1 lt.24
  51.4 4.6 %all-to-all-done.1 = f32[4,4,4]{0,2,1:T(4,128)S(1)} async-done(((f32[4,4,4]{0,2,1:T(4,128)}), f32[4,4,4]{0,2,1:T(4,128)S(1)}, u32[]{:S(2)}, u32[]{:S(2)}) %all-to-all-start.1) | async-done | bytes 288 | tf_op jit(solution)/shard_map/all_to_all | solution.py:57
  56.0 0.1 copy.17
  56.1 0.7 mul.27
  56.9 2.0 %copy.19 = f32[64,8,4,512]{3,1,2,0:T(8,128)S(1)} copy(f32[64,8,4,512]{3,2,1,0:T(4,128)S(1)} %bitcast.50) | data formatting | bytes 8388608
  58.9 0.1 copy-done.2
  59.0 1.3 copy-done.4
  60.3 1.6 multiply_convert_fusion
  61.9 1.3 copy-done.3
  63.2 0.0 copy-done.7
  63.2 1.4 fusion.10
  64.6 0.0 reduce-scatter.2.cloned.1.call-update
  64.7 0.0 all-reduce.3.cloned.1.call-start
  64.7 2.3 %fusion.11 = f32[2048,128]{1,0:T(8,128)S(1)} fusion(bf16[512,2048]{1,0:T(8,128)(2,1)} %copy-done.3, bf16[512,128]{1,0:T(8,128)(2,1)S(1)} %all_gather.3), kind=kOutput, calls=%fused_computation.31 | convolution fusion | flops 268435456 | bytes 3276800 | tf_op jit(solution)/shard_map/dot_general | solution.py:59
  67.0 0.0 copy-start.5
  67.0 1.0 copy-done.5
  68.0 0.6 fusion.1
  68.6 19.9 %reduce-scatter.2.cloned.1.call-done = f32[128,128]{1,0:T(8,128)} async-done(((f32[512,128]{1,0:T(8,128)}), f32[128,128]{1,0:T(8,128)}) %reduce-scatter.2.cloned.1.call-update) | async-done | bytes 65552 | tf_op jit(solution)/shard_map/reduce_scatter | solution.py:60
  88.5 1.9 fusion
  90.5 0.0 all-reduce.3.cloned.1.call-update
  90.5 0.0 all-reduce.5.cloned.1.call-start
  90.5 56.8 %all-reduce.3.cloned.1.call-done = f32[768,128]{0,1:T(8,128)} async-done(((f32[768,128]{0,1:T(8,128)}), f32[768,128]{0,1:T(8,128)}) %all-reduce.3.cloned.1.call-update) | async-done | bytes 393232 | tf_op jit(solution)/shard_map/psum | solution.py:68
  147.3 0.0 all-reduce.5.cloned.1.call-update
  147.4 14.3 %psum.30 = f32[]{:T(128)} all-reduce(f32[]{:T(128)} %get-tuple-element.14), channel_id=1, replica_groups=mesh['blk'=4,'rep'=8] {'rep'}, use_global_device_ids=true, to_apply=%region_10.11 | all-reduce | flops 1 | bytes 8 | tf_op jit(solution)/shard_map/psum | solution.py:68
  161.7 10.4 %psum.31 = f32[]{:T(128)} all-reduce(f32[]{:T(128)} %psum.30), channel_id=1, replica_groups=mesh['blk'=4,'rep'=8] {'blk'}, use_global_device_ids=true, to_apply=%region_11.12 | all-reduce | flops 1 | bytes 8 | tf_op jit(solution)/shard_map/psum | solution.py:68
  172.8 20.7 %all-reduce.5.cloned.1.call-done = f32[768,128]{0,1:T(8,128)} async-done(((f32[768,128]{0,1:T(8,128)}), f32[768,128]{0,1:T(8,128)}) %all-reduce.5.cloned.1.call-update) | async-done | bytes 393232 | tf_op jit(solution)/shard_map/psum | solution.py:68
  193.5 1.9 copy.14
  (12 shorter events, 0.1 us)
Async XLA Ops:
  7.2 1.9 copy-start
  7.2 3.8 %copy-start.8 = (bf16[768,128]{1,0:T(8,128)(2,1)S(1)}, bf16[768,128]{1,0:T(8,128)(2,1)}, u32[]{:S(2)}) copy-start(bf16[768,128]{1,0:T(8,128)(2,1)} %param.7) | copy-start | bytes 589828
  7.2 3.8 %copy-start.9 = (bf16[1,4,32,768]{3,2,1,0:T(8,128)(2,1)S(1)}, bf16[1,4,32,768]{3,2,1,0:T(8,128)(2,1)}, u32[]{:S(2)}) copy-start(bf16[1,4,32,768]{3,2,1,0:T(8,128)(2,1)} %param.4) | copy-start | bytes 589828
  11.0 10.2 %copy-start.6 = (bf16[2048,128]{1,0:T(8,128)(2,1)}, bf16[2048,128]{1,0:T(8,128)(2,1)S(1)}, u32[]{:S(2)}) copy-start(bf16[2048,128]{1,0:T(8,128)(2,1)S(1)} %convolution_convert_fusion) | copy-start | bytes 1572868
  23.8 6.0 %copy-start.11 = (s32[1,4]{1,0:T(1,128)S(1)}, s32[1,4]{1,0:T(1,128)}, u32[]{:S(2)}) copy-start(s32[1,4]{1,0:T(1,128)} %param.6) | copy-start | bytes 52
  29.8 3.4 %copy-start.1 = (f32[512,4,512]{2,1,0:T(4,128)S(1)}, f32[512,4,512]{2,1,0:T(4,128)}, u32[]{:S(2)}) copy-start(f32[512,4,512]{2,1,0:T(4,128)} %div.19) | copy-start | bytes 12582916
  36.7 9.0 %all-to-all-start = ((f32[4,4,4]{1,2,0:T(4,128)}), f32[4,4,4]{1,2,0:T(4,128)S(1)}, u32[]{:S(2)}, u32[]{:S(2)}) async-start(f32[4,4,4]{1,2,0:T(4,128)} %copy.11), calls=%async_computation | async-start | bytes 16384 | tf_op jit(solution)/shard_map/all_to_all | solution.py:55
  41.8 4.0 %copy-start.10 = (s32[4,4]{1,0:T(4,128)S(1)}, s32[4,4]{1,0:T(4,128)}, u32[]{:S(2)}) copy-start(s32[4,4]{1,0:T(4,128)} %multiply_add_fusion) | copy-start | bytes 196
  41.8 4.0 %copy-start.13 = (s32[4]{0:T(128)S(1)}, s32[4]{0:T(128)}, u32[]{:S(2)}) copy-start(s32[4]{0:T(128)} %iota_add_fusion) | copy-start | bytes 52
  41.8 9.5 %copy-start.12 = (s32[1,4]{1,0:T(1,128)S(1)}, s32[1,4]{1,0:T(1,128)}, u32[]{:S(2)}) copy-start(s32[1,4]{1,0:T(1,128)} %param.6) | copy-start | bytes 52
  47.1 8.8 %all-to-all-start.1 = ((f32[4,4,4]{0,2,1:T(4,128)}), f32[4,4,4]{0,2,1:T(4,128)S(1)}, u32[]{:S(2)}, u32[]{:S(2)}) async-start(f32[4,4,4]{0,2,1:T(4,128)} %fusion.5), calls=%async_computation.1 | async-start | bytes 16384 | tf_op jit(solution)/shard_map/all_to_all | solution.py:57
  51.3 37.2 %reduce-scatter.2.cloned.1.call-start = ((), (), s32[]{:S(2)}) async-start(), calls=%async_computation.3 | async-start | bytes 327680 | tf_op jit(solution)/shard_map/reduce_scatter | solution.py:60
  56.8 2.2 %copy-start.2 = (f32[512,2048]{1,0:T(8,128)S(1)}, f32[512,2048]{1,0:T(8,128)}, u32[]{:S(2)}) copy-start(f32[512,2048]{1,0:T(8,128)} %convolution_multiply_fusion) | copy-start | bytes 12582916
  56.8 3.5 %copy-start.4 = (f32[64,8,4,512]{3,1,2,0:T(8,128)S(1)}, f32[64,8,4,512]{3,1,2,0:T(8,128)}, u32[]{:S(2)}) copy-start(f32[64,8,4,512]{3,1,2,0:T(8,128)} %copy.21) | copy-start | bytes 12582916
  60.3 2.9 %copy-start.7 = (bf16[2048,128]{1,0:T(8,128)(2,1)S(1)}, bf16[2048,128]{1,0:T(8,128)(2,1)}, u32[]{:S(2)}) copy-start(bf16[2048,128]{1,0:T(8,128)(2,1)} %copy-done.6) | copy-start | bytes 1572868
  61.9 1.4 copy-start.3
  64.7 82.7 %all-reduce.3.cloned.1.call-start = ((), (), s32[]{:S(2)}) async-start(), calls=%async_computation.4 | async-start | bytes 786432 | tf_op jit(solution)/shard_map/psum | solution.py:68
  67.0 1.0 copy-start.5
  90.5 103.0 %all-reduce.5.cloned.1.call-start = ((), (), s32[]{:S(2)}) async-start(), calls=%async_computation.5 | async-start | bytes 786432 | tf_op jit(solution)/shard_map/psum | solution.py:68
Sparse Core Ops, SparseCore 0:
  64.8 23.6 reduce-scatter.1
  91.4 55.8 all-reduce.2
  150.3 43.1 all-reduce.4
